TPU v7x, 256 devices: a whole 4x4x8 slice. The times are simulated.
256 devices in a mesh: mass: 32 (over x, z), sub: 8 (over y, core).
Axes of the slice: x: 4, y: 4, z: 8, core: 2. Of those that a mesh axis runs over, the one named last changes fastest.
Arguments:
- spectra: bfloat16 [32768, 4096], P(('mass', 'sub')), may hold values from -6 to 6
- w_in: bfloat16 [4096, 2048], P(None, 'sub'), may hold values from -0.09375 to 0.09375
- w_out: bfloat16 [2048, 512], P('sub'), may hold values from -0.125 to 0.125
- partner_rows: int32 [32, 8, 32, 8], P('mass', 'sub'), may hold values from 0 to 127
- pair_counts: int32 [32, 8, 32], P('mass', 'sub'), may hold values from 0 to 8, as said below
- pair_labels: int32 [32, 8, 32, 8], P('mass', 'sub'), may hold values from 0 to 1, as said below
Outputs:
- grad_in: float32 [4096, 2048], P('mass', 'sub')
- grad_out_t: float32 [512, 2048], P('mass', 'sub')
Inputs may be any that keep to these rules, and one draw needn't show every extreme that they name: pair_counts[m, s, q] equals pair_counts[q, s, m], is 0 for q = m, and at most 8; some count equals 8. pair_labels[m, s, q, c] equals pair_labels[q, s, m, c] for q != m.
All inputs are finite; a program needn't handle non-finite values.
Results may differ from a plain program's by a relative error of at most 0.0053.
Values may be sent and summed in bfloat16 or wider, within the bound.
A program may use at most 64 MiB of HBM per device.

v0:
```python
import jax
import jax.numpy as jnp
from jax import lax
from jax.sharding import PartitionSpec as P


def per_device(spectra, w_in, w_out, partner_rows, pair_counts, pair_labels):
    own_rows = spectra.shape[0]
    peers = partner_rows.shape[2]
    slots = partner_rows.shape[3]
    shard_rows = lax.all_gather(spectra, "sub", axis=0, tiled=True)
    pre = jnp.dot(shard_rows, w_in, preferred_element_type=jnp.float32)
    hidden = jax.nn.silu(pre).astype(jnp.bfloat16)
    embed = lax.psum_scatter(
        jnp.dot(hidden, w_out, preferred_element_type=jnp.float32),
        "sub",
        scatter_dimension=0,
        tiled=True,
    )
    norm = jnp.sqrt(jnp.sum(embed * embed, axis=-1, keepdims=True) + 1e-06)
    unit = embed / norm
    unit_b = unit.astype(jnp.bfloat16)
    flat_rows = partner_rows.reshape(peers * slots)
    selector = flat_rows[:, None] == jnp.arange(own_rows, dtype=jnp.int32)[None, :]
    mine = jnp.dot(
        selector.astype(jnp.bfloat16), unit_b, preferred_element_type=jnp.float32
    ).astype(jnp.bfloat16)
    outgoing = mine.reshape(peers, slots, mine.shape[1])
    incoming = lax.all_to_all(outgoing, "mass", split_axis=0, concat_axis=0, tiled=True)
    theirs = incoming.astype(jnp.float32)
    sim = jnp.sum(outgoing.astype(jnp.float32) * theirs, axis=-1)
    valid = jnp.arange(slots, dtype=jnp.int32)[None, :] < pair_counts.reshape(peers)[:, None]
    labels = pair_labels.reshape(peers, slots).astype(jnp.float32)
    coef = jnp.where(valid, 2.0 * (sim - labels), jnp.float32(0.0))
    weighted = (coef[..., None] * theirs).reshape(peers * slots, theirs.shape[2])
    grad_unit = lax.dot_general(
        selector.astype(jnp.float32),
        weighted,
        (((0,), (0,)), ((), ())),
        precision=lax.Precision.HIGHEST,
    )
    along = jnp.sum(unit * grad_unit, axis=-1, keepdims=True)
    grad_embed = ((grad_unit - unit * along) / norm).astype(jnp.bfloat16)
    grad_rows = lax.all_gather(grad_embed, "sub", axis=0, tiled=True)
    back = lax.dot_general(
        grad_rows, w_out, (((1,), (1,)), ((), ())), preferred_element_type=jnp.float32
    )
    gate = jax.nn.sigmoid(pre)
    grad_pre = (back * gate * (1.0 + pre * (1.0 - gate))).astype(jnp.bfloat16)
    out_part = lax.dot_general(
        grad_rows, hidden, (((0,), (0,)), ((), ())), preferred_element_type=jnp.float32
    )
    in_part = lax.dot_general(
        shard_rows, grad_pre, (((0,), (0,)), ((), ())), preferred_element_type=jnp.float32
    )
    n_mass = peers
    in_rows = in_part.shape[0] // n_mass
    out_rows = out_part.shape[0] // n_mass
    partial = jnp.concatenate(
        [
            in_part.reshape(n_mass, in_rows, in_part.shape[1]),
            out_part.reshape(n_mass, out_rows, out_part.shape[1]),
        ],
        axis=1,
    ).astype(jnp.bfloat16)
    summed = jnp.sum(
        lax.all_to_all(partial, "mass", split_axis=0, concat_axis=0, tiled=True).astype(
            jnp.float32
        ),
        axis=0,
    )
    grad_in, grad_out_t = (summed[:in_rows], summed[in_rows:])
    return (grad_in, grad_out_t)


def solution(mesh):
    placed = (
        P(("mass", "sub"), None),
        P(None, "sub"),
        P("sub", None),
        P("mass", "sub", None, None),
        P("mass", "sub", None),
        P("mass", "sub", None, None),
    )
    return jax.shard_map(
        per_device,
        mesh=mesh,
        in_specs=placed,
        out_specs=(P("mass", "sub"), P("mass", "sub")),
        check_vma=False,
    )
```

profile of v0, /device:TPU:32, one launch (start us, length us, event | category | flops | bytes accessed | tf_op | source)
XLA Modules:
  0.0 248.9 jit_solution(8469015729756273993)
XLA Ops:
  7.2 0.0 copy-start
  7.2 0.0 all-gather.3.cloned.1.call-start
  7.2 0.7 all-gather.3.cloned.1.call-update
  7.9 0.0 reduce-scatter.2.cloned.1.call-start
  8.0 56.8 %all-gather.3.cloned.1.call-done = bf16[1024,4096]{1,0:T(8,128)(2,1)} async-done(((bf16[128,4096]{1,0:T(8,128)(2,1)}), bf16[1024,4096]{1,0:T(8,128)(2,1)}) %all-gather.3.cloned.1.call-update) | async-done | bytes 8388624 | tf_op jit(solution)/shard_map/all_gather | solution.py:11
  64.8 5.7 %fusion.20 = f32[1024,256]{1,0:T(8,128)S(1)} fusion(bf16[1024,4096]{1,0:T(8,128)(2,1)} %all-gather.3.cloned.1.call-done, bf16[4096,256]{1,0:T(8,128)(2,1)S(1)} %copy-done), kind=kOutput, calls=%fused_computation.37 | convolution fusion | flops 2147483648 | bytes 11534336 | tf_op jit(solution)/shard_map/dot_general | solution.py:12
  70.5 1.0 copy-done.8
  71.5 1.8 fusion.19
  73.3 0.0 reduce-scatter.2.cloned.1.call-update
  73.4 0.1 copy.13
  73.4 0.1 eq.15
  73.5 36.3 %reduce-scatter.2.cloned.1.call-done = f32[128,512]{1,0:T(8,128)} async-done(((f32[1024,512]{1,0:T(8,128)}), f32[128,512]{1,0:T(8,128)}) %reduce-scatter.2.cloned.1.call-update) | async-done | bytes 262160 | tf_op jit(solution)/shard_map/reduce_scatter | solution.py:14
  109.9 1.1 multiply_reduce_fusion.1
  111.0 2.0 fusion.3
  113.0 10.1 %all-to-all-start = ((bf16[32,8,512]{2,1,0:T(8,128)(2,1)}), bf16[32,8,512]{2,1,0:T(8,128)(2,1)S(1)}, u32[]{:S(2)}, u32[]{:S(2)}) async-start(bf16[32,8,512]{2,1,0:T(8,128)(2,1)} %fusion.3), calls=%async_computation.1 | async-start | bytes 524288 | tf_op jit(solution)/shard_map/all_to_all | solution.py:29
  123.1 0.0 all-gather.5.cloned.1.call-start
  123.1 0.1 copy.14
  123.2 10.9 %all-to-all-done = bf16[32,8,512]{2,1,0:T(8,128)(2,1)S(1)} async-done(((bf16[32,8,512]{2,1,0:T(8,128)(2,1)}), bf16[32,8,512]{2,1,0:T(8,128)(2,1)S(1)}, u32[]{:S(2)}, u32[]{:S(2)}) %all-to-all-start) | async-done | bytes 262176 | tf_op jit(solution)/shard_map/all_to_all | solution.py:29
  134.1 1.1 fusion.7
  135.2 0.1 fusion.17
  135.3 1.5 multiply_reduce_fusion
  136.8 0.8 divide_convert_fusion
  137.6 0.0 all-gather.5.cloned.1.call-update
  137.6 20.8 %all-gather.5.cloned.1.call-done = bf16[1024,512]{1,0:T(8,128)(2,1)} async-done(((bf16[128,512]{1,0:T(8,128)(2,1)}), bf16[1024,512]{1,0:T(8,128)(2,1)}) %all-gather.5.cloned.1.call-update) | async-done | bytes 1048592 | tf_op jit(solution)/shard_map/all_gather | solution.py:44
  158.4 8.6 %fusion = bf16[4096,256]{0,1:T(8,128)(2,1)} fusion(bf16[1024,4096]{1,0:T(8,128)(2,1)} %all-gather.3.cloned.1.call-done, bf16[1024,512]{1,0:T(8,128)(2,1)} %all-gather.5.cloned.1.call-done, bf16[256,512]{1,0:T(8,128)(2,1)S(1)} %copy-done.7, f32[1024,256]{1,0:T(8,128)} %copy-done.8), kind=kOutput, calls=%fused_computation.1 | convolution fusion | flops 2419326976 | bytes 12845056 | tf_op jit(solution)/shard_map/dot_general | solution.py:53
  167.0 4.2 %copy.19 = bf16[4096,256]{1,0:T(8,128)(2,1)} copy(bf16[4096,256]{0,1:T(8,128)(2,1)} %fusion) | data formatting | bytes 4194304 | tf_op jit(solution)/shard_map/reshape | solution.py:61
  171.2 1.9 convolution_convert_fusion.1
  173.1 0.2 pad_maximum_fusion
  173.3 67.5 %all_to_all.10 = bf16[32,144,256]{2,1,0:T(8,128)(2,1)S(1)} all-to-all(bf16[32,144,256]{2,1,0:T(8,128)(2,1)S(1)} %pad_maximum_fusion), channel_id=1, replica_groups=mesh['mass'=32,'sub'=8] {'mass'}, dimensions={0} | all-to-all | bytes 4718592 | tf_op jit(solution)/shard_map/all_to_all | solution.py:67
  240.8 0.3 convert_reduce_fusion
  241.1 0.6 slice.9
  241.7 0.7 slice.8
  (17 shorter events, 0.0 us)
Async XLA Ops:
  7.2 57.6 %copy-start = (bf16[4096,256]{1,0:T(8,128)(2,1)S(1)}, bf16[4096,256]{1,0:T(8,128)(2,1)}, u32[]{:S(2)}) copy-start(bf16[4096,256]{1,0:T(8,128)(2,1)} %param.7) | copy-start | bytes 6291460
  7.2 57.6 %all-gather.3.cloned.1.call-start = ((), (), s32[]{:S(2)}) async-start(), calls=%async_computation.3 | async-start | bytes 9437184 | tf_op jit(solution)/shard_map/all_gather | solution.py:11
  7.9 63.6 %copy-start.7 = (bf16[256,512]{1,0:T(8,128)(2,1)S(1)}, bf16[256,512]{1,0:T(8,128)(2,1)}, u32[]{:S(2)}) copy-start(bf16[256,512]{1,0:T(8,128)(2,1)} %param.8) | copy-start | bytes 786436
  7.9 102.0 %reduce-scatter.2.cloned.1.call-start = ((), (), s32[]{:S(2)}) async-start(), calls=%async_computation.4 | async-start | bytes 2359296 | tf_op jit(solution)/shard_map/reduce_scatter | solution.py:14
  70.5 1.0 copy-start.8
  71.5 1.9 copy-start.3
  73.3 49.8 %copy-start.4 = (s32[1,1,32,8]{2,3,1,0:T(8,128)S(1)}, s32[1,1,32,8]{2,3,1,0:T(8,128)}, u32[]{:S(2)}) copy-start(s32[1,1,32,8]{2,3,1,0:T(8,128)} %param.11) | copy-start | bytes 3076
  73.3 61.9 %copy-start.5 = (s32[1,1,32]{2,1,0:T(1,128)S(1)}, s32[1,1,32]{2,1,0:T(1,128)}, u32[]{:S(2)}) copy-start(s32[1,1,32]{2,1,0:T(1,128)} %param.10) | copy-start | bytes 388
  109.9 26.9 %copy-start.2 = (f32[128,512]{1,0:T(8,128)S(1)}, f32[128,512]{1,0:T(8,128)}, u32[]{:S(2)}) copy-start(f32[128,512]{1,0:T(8,128)} %reduce-scatter.2.cloned.1.call-done) | copy-start | bytes 786436
  113.0 21.1 %all-to-all-start = ((bf16[32,8,512]{2,1,0:T(8,128)(2,1)}), bf16[32,8,512]{2,1,0:T(8,128)(2,1)S(1)}, u32[]{:S(2)}, u32[]{:S(2)}) async-start(bf16[32,8,512]{2,1,0:T(8,128)(2,1)} %fusion.3), calls=%async_computation.1 | async-start | bytes 524288 | tf_op jit(solution)/shard_map/all_to_all | solution.py:29
  123.1 35.3 %all-gather.5.cloned.1.call-start = ((), (), s32[]{:S(2)}) async-start(), calls=%async_computation.5 | async-start | bytes 1179648 | tf_op jit(solution)/shard_map/all_gather | solution.py:44
  167.0 4.2 %copy-start.6 = (bf16[1024,512]{1,0:T(8,128)(2,1)S(1)}, bf16[1024,512]{1,0:T(8,128)(2,1)}, u32[]{:S(2)}) copy-start(bf16[1024,512]{1,0:T(8,128)(2,1)} %all-gather.5.cloned.1.call-done) | copy-start | bytes 3145732
  171.2 2.0 copy-start.1
Sparse Core Ops, SparseCore 0:
  9.9 54.8 all-gather.2
  73.5 36.3 reduce-scatter.1
  137.7 20.6 all-gather.4
where the time goes:
time: 249 us
  waiting for transfers between devices  126 us (51%)
  blocking collectives  67.5 us (27%)
  matrix products  21.5 us (9%)
  between operations  13.9 us (6%)
  starting transfers between devices  10.2 us (4%)
  local copies, waits for them, and re-layouts  6.69 us (3%)
  other arithmetic  3.58 us (1%)
    all_to_all x1, blocking collectives, per_device(): lax.all_to_all(partial, 'mass', split_axis=0, concat_axis=0, tiled=True)  67.5 us
    all_gather x1, waiting for transfers between devices, per_device(): shard_rows = lax.all_gather(spectra, 'sub', axis=0, tiled=True)  56.8 us
    reduce_scatter x1, waiting for transfers between devices, per_device(): lax.psum_scatter(jnp.dot(hidden, w_out, preferred_element_type=jnp.float3...  36.3 us
    all_gather x1, waiting for transfers between devices, per_device(): grad_rows = lax.all_gather(grad_embed, 'sub', axis=0, tiled=True)  20.8 us
    all_to_all x1, waiting for transfers between devices, per_device(): lax.all_to_all(outgoing, 'mass', split_axis=0, concat_axis=0, tiled=True)  10.9 us
    all_to_all x1, starting transfers between devices, per_device(): lax.all_to_all(outgoing, 'mass', split_axis=0, concat_axis=0, tiled=True)  10.1 us
    dot_general x1, matrix products, per_device(): lax.dot_general(shard_rows, grad_pre, (((0,), (0,)), ((), ())), preferred...  8.59 us
    dot_general x1, matrix products, per_device(): pre = jnp.dot(shard_rows, w_in, preferred_element_type=jnp.float32)  5.71 us
  transfers between devices with their start and end apart: 4, of which 4 were waited for; matrix products, arithmetic and copies ran while one was open for 0% of the time, Pallas kernels for 0%

commit v1 on v0

--- a/solution.py
+++ b/solution.py
@@ -41,7 +41,9 @@
     )
     along = jnp.sum(unit * grad_unit, axis=-1, keepdims=True)
     grad_embed = ((grad_unit - unit * along) / norm).astype(jnp.bfloat16)
-    grad_rows = lax.all_gather(grad_embed, "sub", axis=0, tiled=True)
+    grad_rows = jnp.concatenate(
+        lax.all_to_all(jnp.stack([grad_embed] * lax.axis_size("sub")), "sub", 0, 0), axis=0
+    )
     back = lax.dot_general(
         grad_rows, w_out, (((1,), (1,)), ((), ())), preferred_element_type=jnp.float32
     )

time: 249 us -> 244 us (0.980)
  waiting for transfers between devices: 126 us -> 105 us
  blocking collectives: 67.5 us -> 80.4 us
  local copies, waits for them, and re-layouts: 6.69 us -> 9.65 us
    all_gather x1 -> x0, waiting for transfers between devices: 20.8 us -> none  [per_device(): grad_rows = lax.all_gather(grad_embed, 'sub', axis=0, tiled=True)]
    all_to_all x0 -> x1, blocking collectives: none -> 19.2 us  [per_device(): lax.all_to_all(jnp.stack([grad_embed] * lax.axis_size('sub')), 'sub', 0, 0)]
    all_to_all x1, blocking collectives: 67.5 us -> 61.2 us  [per_device(): lax.all_to_all(partial, 'mass', split_axis=0, concat_axis=0, tiled=True)]
  transfers between devices with their start and end apart: 4 -> 3, of which waited for: 4 -> 3; matrix products, arithmetic and copies ran while one was open for 0% -> 0% of each run, Pallas kernels for 0% -> 0%
where the time goes in v1:
time: 244 us
  waiting for transfers between devices  105 us (43%)
  blocking collectives  80.4 us (33%)
  matrix products  21.5 us (9%)
  between operations  14.2 us (6%)
  starting transfers between devices  10.2 us (4%)
  local copies, waits for them, and re-layouts  9.65 us (4%)
  other arithmetic  2.92 us (1%)
    all_to_all x1, blocking collectives, per_device(): lax.all_to_all(partial, 'mass', split_axis=0, concat_axis=0, tiled=True)  61.2 us
    all_gather x1, waiting for transfers between devices, per_device(): shard_rows = lax.all_gather(spectra, 'sub', axis=0, tiled=True)  56.8 us
    reduce_scatter x1, waiting for transfers between devices, per_device(): lax.psum_scatter(jnp.dot(hidden, w_out, preferred_element_type=jnp.float3...  36.3 us
    all_to_all x1, blocking collectives, per_device(): lax.all_to_all(jnp.stack([grad_embed] * lax.axis_size('sub')), 'sub', 0, 0)  19.2 us
    all_to_all x1, waiting for transfers between devices, per_device(): lax.all_to_all(outgoing, 'mass', split_axis=0, concat_axis=0, tiled=True)  11 us
    all_to_all x1, starting transfers between devices, per_device(): lax.all_to_all(outgoing, 'mass', split_axis=0, concat_axis=0, tiled=True)  10.1 us
    dot_general x1, matrix products, per_device(): lax.dot_general(shard_rows, grad_pre, (((0,), (0,)), ((), ())), preferred...  8.29 us
    dot_general x1, matrix products, per_device(): pre = jnp.dot(shard_rows, w_in, preferred_element_type=jnp.float32)  5.71 us
  transfers between devices with their start and end apart: 3, of which 3 were waited for; matrix products, arithmetic and copies ran while one was open for 0% of the time, Pallas kernels for 0%

profile of v1, /device:TPU:32, one launch (start us, length us, event | category | flops | bytes accessed | tf_op | source)
XLA Modules:
  0.0 243.7 jit_solution(2869712950035792500)
XLA Ops:
  7.2 0.0 all-gather.2.cloned.1.call-start
  7.2 0.7 all-gather.2.cloned.1.call-update
  7.9 0.0 reduce-scatter.2.cloned.1.call-start
  8.0 56.8 %all-gather.2.cloned.1.call-done = bf16[1024,4096]{1,0:T(8,128)(2,1)} async-done(((bf16[128,4096]{1,0:T(8,128)(2,1)}), bf16[1024,4096]{1,0:T(8,128)(2,1)}) %all-gather.2.cloned.1.call-update) | async-done | bytes 8388624 | tf_op jit(solution)/shard_map/all_gather | solution.py:11
  64.8 5.7 %fusion.21 = f32[1024,256]{1,0:T(8,128)S(1)} fusion(bf16[1024,4096]{1,0:T(8,128)(2,1)} %all-gather.2.cloned.1.call-done, bf16[4096,256]{1,0:T(8,128)(2,1)S(1)} %copy-done), kind=kOutput, calls=%fused_computation.38 | convolution fusion | flops 2147483648 | bytes 11534336 | tf_op jit(solution)/shard_map/dot_general | solution.py:12
  70.5 1.0 copy-done.7
  71.5 1.8 fusion.20
  73.4 0.1 copy.22
  73.5 0.1 eq.15
  73.6 36.3 %reduce-scatter.2.cloned.1.call-done = f32[128,512]{1,0:T(8,128)} async-done(((f32[1024,512]{1,0:T(8,128)}), f32[128,512]{1,0:T(8,128)}) %reduce-scatter.2.cloned.1.call-update) | async-done | bytes 262160 | tf_op jit(solution)/shard_map/reduce_scatter | solution.py:14
  109.9 1.1 multiply_reduce_fusion.1
  111.0 2.0 fusion.3
  113.0 10.1 %all-to-all-start = ((bf16[32,8,512]{2,1,0:T(8,128)(2,1)}), bf16[32,8,512]{2,1,0:T(8,128)(2,1)S(1)}, u32[]{:S(2)}, u32[]{:S(2)}) async-start(bf16[32,8,512]{2,1,0:T(8,128)(2,1)} %fusion.3), calls=%async_computation.1 | async-start | bytes 524288 | tf_op jit(solution)/shard_map/all_to_all | solution.py:29
  123.1 0.1 copy.23
  123.2 11.0 %all-to-all-done = bf16[32,8,512]{2,1,0:T(8,128)(2,1)S(1)} async-done(((bf16[32,8,512]{2,1,0:T(8,128)(2,1)}), bf16[32,8,512]{2,1,0:T(8,128)(2,1)S(1)}, u32[]{:S(2)}, u32[]{:S(2)}) %all-to-all-start) | async-done | bytes 262176 | tf_op jit(solution)/shard_map/all_to_all | solution.py:29
  134.1 1.1 fusion.7
  135.2 0.1 fusion.18
  135.3 1.5 multiply_reduce_fusion
  136.8 0.1 divide_convert_fusion
  136.9 0.1 copy.24
  137.0 0.1 stack.2
  137.2 19.2 %all_to_all.15 = bf16[8,128,512]{1,2,0:T(8,128)(2,1)} all-to-all(bf16[8,128,512]{1,2,0:T(8,128)(2,1)S(1)} %stack.2), channel_id=1, replica_groups=mesh['mass'=32,'sub'=8] {'sub'}, dimensions={0} | all-to-all | bytes 2097152 | tf_op jit(solution)/shard_map/all_to_all | solution.py:45
  156.4 1.5 copy.25
  157.9 8.3 %fusion = bf16[4096,256]{0,1:T(8,128)(2,1)} fusion(bf16[1024,4096]{1,0:T(8,128)(2,1)} %all-gather.2.cloned.1.call-done, bf16[1024,512]{1,0:T(8,128)(2,1)S(1)} %bitcast.34, bf16[256,512]{1,0:T(8,128)(2,1)S(1)} %copy-done.6, f32[1024,256]{1,0:T(8,128)} %copy-done.7), kind=kOutput, calls=%fused_computation.1 | convolution fusion | flops 2419326976 | bytes 12845056 | tf_op jit(solution)/shard_map/dot_general | solution.py:55
  166.2 4.1 %copy.31 = bf16[4096,256]{1,0:T(8,128)(2,1)} copy(bf16[4096,256]{0,1:T(8,128)(2,1)} %fusion) | data formatting | bytes 4194304 | tf_op jit(solution)/shard_map/reshape | solution.py:63
  170.3 1.3 copy.26
  171.6 2.2 convolution_convert_fusion.1
  173.9 0.2 pad_maximum_fusion
  174.0 61.2 %all_to_all.16 = bf16[32,144,256]{2,1,0:T(8,128)(2,1)S(1)} all-to-all(bf16[32,144,256]{2,1,0:T(8,128)(2,1)S(1)} %pad_maximum_fusion), channel_id=1, replica_groups=mesh['mass'=32,'sub'=8] {'mass'}, dimensions={0} | all-to-all | bytes 4718592 | tf_op jit(solution)/shard_map/all_to_all | solution.py:69
  235.2 0.3 convert_reduce_fusion
  235.6 0.6 slice.9
  236.2 0.7 slice.8
  (17 shorter events, 0.1 us)
Async XLA Ops:
  7.2 57.6 %copy-start = (bf16[4096,256]{1,0:T(8,128)(2,1)S(1)}, bf16[4096,256]{1,0:T(8,128)(2,1)}, u32[]{:S(2)}) copy-start(bf16[4096,256]{1,0:T(8,128)(2,1)} %param.7) | copy-start | bytes 6291460
  7.2 57.6 %all-gather.2.cloned.1.call-start = ((), (), s32[]{:S(2)}) async-start(), calls=%async_computation.4 | async-start | bytes 9437184 | tf_op jit(solution)/shard_map/all_gather | solution.py:11
  7.9 63.6 %copy-start.6 = (bf16[256,512]{1,0:T(8,128)(2,1)S(1)}, bf16[256,512]{1,0:T(8,128)(2,1)}, u32[]{:S(2)}) copy-start(bf16[256,512]{1,0:T(8,128)(2,1)} %param.8) | copy-start | bytes 786436
  7.9 101.9 %reduce-scatter.2.cloned.1.call-start = ((), (), s32[]{:S(2)}) async-start(), calls=%async_computation.5 | async-start | bytes 2359296 | tf_op jit(solution)/shard_map/reduce_scatter | solution.py:14
  70.5 1.0 copy-start.7
  71.5 1.9 copy-start.3
  73.3 49.7 %copy-start.4 = (s32[1,1,32,8]{2,3,1,0:T(8,128)S(1)}, s32[1,1,32,8]{2,3,1,0:T(8,128)}, u32[]{:S(2)}) copy-start(s32[1,1,32,8]{2,3,1,0:T(8,128)} %param.11) | copy-start | bytes 3076
  73.4 61.9 %copy-start.5 = (s32[1,1,32]{2,1,0:T(1,128)S(1)}, s32[1,1,32]{2,1,0:T(1,128)}, u32[]{:S(2)}) copy-start(s32[1,1,32]{2,1,0:T(1,128)} %param.10) | copy-start | bytes 388
  109.9 26.9 %copy-start.2 = (f32[128,512]{1,0:T(8,128)S(1)}, f32[128,512]{1,0:T(8,128)}, u32[]{:S(2)}) copy-start(f32[128,512]{1,0:T(8,128)} %reduce-scatter.2.cloned.1.call-done) | copy-start | bytes 786436
  113.0 21.1 %all-to-all-start = ((bf16[32,8,512]{2,1,0:T(8,128)(2,1)}), bf16[32,8,512]{2,1,0:T(8,128)(2,1)S(1)}, u32[]{:S(2)}, u32[]{:S(2)}) async-start(bf16[32,8,512]{2,1,0:T(8,128)(2,1)} %fusion.3), calls=%async_computation.1 | async-start | bytes 524288 | tf_op jit(solution)/shard_map/all_to_all | solution.py:29
  171.6 2.3 copy-start.1
Sparse Core Ops, SparseCore 0:
  9.9 54.8 all-gather.1
  73.5 36.3 reduce-scatter.1
